TPU v7x, 256 devices: a whole 4x4x8 slice. The times are simulated.
256 devices in a mesh: gx: 16 (over z_hi, y, core), gy: 16 (over z_lo, x).
Axes of the slice: x: 4, y: 4, z: 8 (z_hi: 2, z_lo: 4; z = z_hi * 4 + z_lo), core: 2. Of those that a mesh axis runs over, the one named last changes fastest.
Arguments:
- skip_input: bfloat16 [32, 64, 4096], P(None, 'gx', 'gy'), may hold values from -6 to 6
- w_encoder: bfloat16 [64, 864], replicated, may hold values from -0.625 to 0.625
- w_bottom: bfloat16 [128, 1728], P('gx'), may hold values from -0.3125 to 0.3125
- w_middle: bfloat16 [64, 5184], replicated, may hold values from -0.15625 to 0.15625
- w_upper: bfloat16 [32, 2592], replicated, may hold values from -0.21875 to 0.21875
- cotangent: bfloat16 [32, 64, 4096], P(None, 'gx', 'gy'), may hold values from -6 to 6
Outputs:
- features: bfloat16 [32, 64, 4096], P(None, 'gx', 'gy')
- grad_skip: bfloat16 [32, 64, 4096], P(None, 'gx', 'gy')
- grad_encoder: float32 [64, 864], replicated
- grad_bottom: float32 [128, 1728], P('gx')
- grad_middle: float32 [64, 5184], replicated
- grad_upper: float32 [32, 2592], replicated
All inputs are finite; a program needn't handle non-finite values.
Results may differ from a plain program's by a relative error of at most 0.017.
Values may be sent and summed in bfloat16 or wider, within the bound.
No kernel may reach another device: no remote copies, remote signals or barrier semaphores. Data moves between devices by JAX's collectives and lax.ppermute only.
A program may use at most 64 MiB of HBM per device.

v0:
```python
import math
import jax
import jax.numpy as jnp
from jax import lax
from jax.sharding import PartitionSpec as P

Z = 16


def extended_2(cells, sides, width):
    for axis, dim in sides:
        count = lax.axis_size(axis)
        ends = count - 1
        head = lax.slice_in_dim(cells, 0, width, axis=dim)
        tail = lax.slice_in_dim(cells, cells.shape[dim] - width, cells.shape[dim], axis=dim)
        cells = jnp.concatenate(
            [
                lax.ppermute(tail, axis, [(i, (i + 1) % count) for i in range(ends)]),
                cells,
                lax.ppermute(head, axis, [((i + 1) % count, i) for i in range(ends)]),
            ],
            axis=dim,
        )
    return cells


def z_shift(extended, z_step, z_depth):
    length = extended.shape[2]
    padded = jnp.pad(extended, ((0, 0), (0, 0), (1, 1)))
    shifted = padded[:, :, 1 + z_step : 1 + z_step + length]
    z_index = lax.broadcasted_iota(jnp.int32, (1, 1, length), 2) % z_depth + z_step
    inside = (z_index >= 0) & (z_index < z_depth)
    return jnp.where(inside, shifted, jnp.zeros_like(shifted))


def tap_piece(shifted_set, a, b, c, row_count, col_count, z_depth, flipped):
    x_off, y_off, z_off = (2 - a, 2 - b, 2 - c) if flipped else (a, b, c)
    source = shifted_set[z_off]
    tap_slice = source[
        :, x_off : x_off + row_count, y_off * z_depth : (y_off + col_count) * z_depth
    ]
    return tap_slice.reshape(source.shape[0], row_count * col_count * z_depth)


def conv_forward(extended, weight, row_count, col_count, z_depth):
    in_chan = extended.shape[0]
    shifted_set = [z_shift(extended, z_step, z_depth) for z_step in (-1, 0, 1)]
    total_sum = jnp.zeros((weight.shape[0], row_count * col_count * z_depth), jnp.float32)
    for a in range(3):
        for b in range(3):
            for c in range(3):
                tap_number = 9 * a + 3 * b + c
                total_sum = total_sum + jnp.dot(
                    weight[:, tap_number * in_chan : (tap_number + 1) * in_chan],
                    tap_piece(shifted_set, a, b, c, row_count, col_count, z_depth, False),
                    preferred_element_type=jnp.float32,
                )
    return total_sum


def conv_backward(extended, weight, row_count, col_count, z_depth):
    in_chan = weight.shape[1] // 27
    shifted_set = [z_shift(extended, z_step, z_depth) for z_step in (-1, 0, 1)]
    total_sum = jnp.zeros((in_chan, row_count * col_count * z_depth), jnp.float32)
    for a in range(3):
        for b in range(3):
            for c in range(3):
                tap_number = 9 * a + 3 * b + c
                total_sum = total_sum + lax.dot_general(
                    weight[:, tap_number * in_chan : (tap_number + 1) * in_chan],
                    tap_piece(shifted_set, a, b, c, row_count, col_count, z_depth, True),
                    (((0,), (0,)), ((), ())),
                    preferred_element_type=jnp.float32,
                )
    return total_sum


def weight_grad(extended, error_flat, row_count, col_count, z_depth):
    shifted_set = [z_shift(extended, z_step, z_depth) for z_step in (-1, 0, 1)]
    blocks = []
    for a in range(3):
        for b in range(3):
            for c in range(3):
                blocks.append(
                    lax.dot_general(
                        error_flat,
                        tap_piece(shifted_set, a, b, c, row_count, col_count, z_depth, False),
                        (((1,), (1,)), ((), ())),
                        preferred_element_type=jnp.float32,
                    )
                )
    return jnp.concatenate(blocks, axis=1)


def pool_mean(values, z_depth):
    channels, row_count, length = values.shape
    col_count = length // z_depth
    shaped = values.astype(jnp.float32).reshape(
        channels, row_count // 2, 2, col_count // 2, 2, z_depth // 2, 2
    )
    return shaped.mean(axis=(2, 4, 6)).reshape(
        channels, row_count // 2, col_count // 2 * (z_depth // 2)
    )


def block_sum(values, z_depth):
    channels, row_count, length = values.shape
    col_count = length // z_depth
    shaped = values.reshape(channels, row_count // 2, 2, col_count // 2, 2, z_depth // 2, 2)
    return shaped.sum(axis=(2, 4, 6)).reshape(
        channels, row_count // 2, col_count // 2 * (z_depth // 2)
    )


def upsample(values, z_depth):
    channels, row_count, length = values.shape
    col_count = length // z_depth
    shaped = values.reshape(channels, row_count, 1, col_count, 1, z_depth, 1)
    shaped = jnp.broadcast_to(shaped, (channels, row_count, 2, col_count, 2, z_depth, 2))
    return shaped.reshape(channels, 2 * row_count, 4 * col_count * z_depth)


def silu_slope(values):
    s_value = jax.nn.sigmoid(values)
    return s_value * (1.0 + values * (1.0 - s_value))


def spatial_halo(values, z_depth):
    widened = extended_2(values, (("gx", 1),), 1)
    return extended_2(widened, (("gy", 2),), z_depth)


def per_device(skip_input, w_encoder, w_bottom, w_middle, w_upper, cotangent):
    top_chan = skip_input.shape[0]
    rows_fine = skip_input.shape[1]
    cols_fine = skip_input.shape[2] // Z
    rows_mid, cols_mid, depth_mid = (rows_fine // 2, cols_fine // 2, Z // 2)
    rows_low, cols_low, depth_low = (rows_fine // 4, cols_fine // 4, Z // 4)
    cells_fine = rows_fine * cols_fine * Z * lax.axis_size("gx") * lax.axis_size("gy")
    scale_fine = 1.0 / math.sqrt(cells_fine)
    scale_mid = 1.0 / math.sqrt(cells_fine // 8)
    scale_low = 1.0 / math.sqrt(cells_fine // 64)
    pool_top = pool_mean(skip_input, Z).astype(jnp.bfloat16)
    ext_pool = spatial_halo(pool_top, depth_mid)
    pre_one = conv_forward(ext_pool, w_encoder, rows_mid, cols_mid, depth_mid)
    act_one = jax.nn.silu(pre_one).astype(jnp.bfloat16).reshape(-1, rows_mid, cols_mid * depth_mid)
    pool_mid = pool_mean(act_one, depth_mid).astype(jnp.bfloat16)
    col_ext = extended_2(pool_mid, (("gy", 2),), depth_low)
    whole_rows = lax.all_gather(col_ext, "gx", axis=1, tiled=True)
    ext_low = jnp.pad(whole_rows, ((0, 0), (1, 1), (0, 0)))
    rows_all = whole_rows.shape[1]
    pre_two = conv_forward(ext_low, w_bottom, rows_all, cols_low, depth_low)
    act_block = (
        jax.nn.silu(pre_two).astype(jnp.bfloat16).reshape(-1, rows_all, cols_low * depth_low)
    )
    act_two = lax.all_to_all(act_block, "gx", split_axis=1, concat_axis=0, tiled=True)
    cat_mid = jnp.concatenate([upsample(act_two, depth_low), act_one], axis=0)
    ext_mid = spatial_halo(cat_mid, depth_mid)
    pre_three = conv_forward(ext_mid, w_middle, rows_mid, cols_mid, depth_mid)
    act_three = (
        jax.nn.silu(pre_three).astype(jnp.bfloat16).reshape(-1, rows_mid, cols_mid * depth_mid)
    )
    cat_top = jnp.concatenate([upsample(act_three, depth_mid), skip_input], axis=0)
    ext_top = spatial_halo(cat_top, Z)
    pre_four = conv_forward(ext_top, w_upper, rows_fine, cols_fine, Z)
    features = (
        jax.nn.silu(pre_four).astype(jnp.bfloat16).reshape(top_chan, rows_fine, cols_fine * Z)
    )
    err_four = (cotangent.reshape(top_chan, -1).astype(jnp.float32) * silu_slope(pre_four)).astype(
        jnp.bfloat16
    )
    local_upper = weight_grad(ext_top, err_four, rows_fine, cols_fine, Z) * scale_fine
    grad_upper = lax.psum(local_upper, ("gx", "gy"))
    dcat_top = conv_backward(
        spatial_halo(err_four.reshape(top_chan, rows_fine, cols_fine * Z), Z),
        w_upper,
        rows_fine,
        cols_fine,
        Z,
    ).reshape(-1, rows_fine, cols_fine * Z)
    mid_chan = act_three.shape[0]
    err_three = (
        block_sum(dcat_top[:mid_chan], Z).reshape(mid_chan, -1) * silu_slope(pre_three)
    ).astype(jnp.bfloat16)
    local_middle = weight_grad(ext_mid, err_three, rows_mid, cols_mid, depth_mid) * scale_mid
    grad_middle = lax.psum(local_middle, ("gx", "gy"))
    dcat_mid = conv_backward(
        spatial_halo(err_three.reshape(mid_chan, rows_mid, cols_mid * depth_mid), depth_mid),
        w_middle,
        rows_mid,
        cols_mid,
        depth_mid,
    ).reshape(-1, rows_mid, cols_mid * depth_mid)
    low_chan = act_two.shape[0]
    dact_two = block_sum(dcat_mid[:low_chan], depth_mid)
    dact_block = lax.all_to_all(dact_two, "gx", split_axis=0, concat_axis=1, tiled=True)
    block_chan = dact_block.shape[0]
    err_two = (dact_block.reshape(block_chan, -1) * silu_slope(pre_two)).astype(jnp.bfloat16)
    part_bottom = weight_grad(ext_low, err_two, rows_all, cols_low, depth_low)
    err_grid = err_two.reshape(block_chan, rows_all, cols_low * depth_low)
    err_cols = extended_2(err_grid, (("gy", 2),), depth_low)
    err_ext = jnp.pad(err_cols, ((0, 0), (1, 1), (0, 0)))
    partial_sum = conv_backward(err_ext, w_bottom, rows_all, cols_low, depth_low).reshape(
        -1, rows_all, cols_low * depth_low
    )
    dpool_mid = lax.psum_scatter(
        partial_sum.astype(jnp.bfloat16), "gx", scatter_dimension=1, tiled=True
    ).astype(jnp.float32)
    grad_bottom = lax.psum((part_bottom * scale_low).astype(jnp.bfloat16), "gy").astype(jnp.float32)
    dact_one = dcat_mid[low_chan:] + upsample(dpool_mid, depth_low) / 8.0
    err_one = (dact_one.reshape(mid_chan, -1) * silu_slope(pre_one)).astype(jnp.bfloat16)
    local_encoder = weight_grad(ext_pool, err_one, rows_mid, cols_mid, depth_mid) * scale_mid
    grad_encoder = lax.psum(local_encoder, ("gx", "gy"))
    dpool_top = conv_backward(
        spatial_halo(err_one.reshape(mid_chan, rows_mid, cols_mid * depth_mid), depth_mid),
        w_encoder,
        rows_mid,
        cols_mid,
        depth_mid,
    ).reshape(-1, rows_mid, cols_mid * depth_mid)
    grad_skip = (dcat_top[mid_chan:] + upsample(dpool_top, depth_mid) / 8.0).astype(jnp.bfloat16)
    return (features, grad_skip, grad_encoder, grad_bottom, grad_middle, grad_upper)


def solution(mesh):
    in_specs = (P(None, "gx", "gy"), P(), P("gx", None), P(), P(), P(None, "gx", "gy"))
    out_specs = (P(None, "gx", "gy"), P(None, "gx", "gy"), P(), P("gx", None), P(), P())
    return jax.shard_map(
        per_device, mesh=mesh, in_specs=in_specs, out_specs=out_specs, check_vma=False
    )
```

profile of v0, /device:TPU:4, one launch (start us, length us, event | category | flops | bytes accessed | tf_op | source)
XLA Modules:
  0.0 701.9 jit_solution(12189707919216640930)
XLA Ops:
  14.8 3.1 collective-permute-start.2
  17.9 2.7 collective-permute-start.3
  34.1 5.8 collective-permute-start.4
  41.9 3.5 collective-permute-done.5
  45.4 33.5 %all_gather.3 = bf16[64,16,24]{0,2,1:T(8,128)(2,1)S(1)} all-gather(bf16[64,1,24]{0,2,1:T(8,128)(2,1)S(1)} %pad_maximum_fusion.21), channel_id=1, replica_groups=mesh['gx'=16,'gy'=16] {'gx'}, dimensions={1}, use_global_device_ids=true | all-gather | bytes 52224 | tf_op jit(solution)/shard_map/all_gather | solution.py:149
  86.0 6.4 all-to-all-start
  92.6 9.9 %all-to-all-done = bf16[8,16,16]{2,0,1:T(8,128)(2,1)S(1)} async-done(((bf16[8,16,16]{2,0,1:T(8,128)(2,1)}), bf16[8,16,16]{2,0,1:T(8,128)(2,1)S(1)}, u32[]{:S(2)}, u32[]{:S(2)}) %all-to-all-start) | async-done | bytes 4128 | tf_op jit(solution)/shard_map/all_to_all | solution.py:156
  108.0 4.2 collective-permute-start.8
  114.2 3.7 collective-permute-done.9
  127.1 3.1 collective-permute-start.10
  134.4 4.1 collective-permute-start.12
  140.6 3.6 collective-permute-done.13
  157.6 3.4 collective-permute-start.14
  165.3 4.1 collective-permute-start.16
  172.7 2.8 collective-permute-done.17
  209.4 3.1 collective-permute-start.18
  217.7 4.0 collective-permute-start.20
  270.0 28.7 %all-to-all-start.1 = ((f32[16,1,128]{2,1,0:T(1,128)}), f32[16,1,128]{2,1,0:T(1,128)S(1)}, u32[]{:S(2)}, u32[]{:S(2)}) async-start(f32[16,1,128]{2,1,0:T(1,128)} %reshape.1246), calls=%async_computation.1 | async-start | bytes 16384 | tf_op jit(solution)/shard_map/all_to_all | solution.py:196
  300.3 8.3 %all-to-all-done.1 = f32[16,1,128]{2,1,0:T(1,128)S(1)} async-done(((f32[16,1,128]{2,1,0:T(1,128)}), f32[16,1,128]{2,1,0:T(1,128)S(1)}, u32[]{:S(2)}, u32[]{:S(2)}) %all-to-all-start.1) | async-done | bytes 8224 | tf_op jit(solution)/shard_map/all_to_all | solution.py:196
  314.0 4.3 collective-permute-start.22
  320.5 3.6 collective-permute-done.23
  335.1 70.2 %psum.29 = bf16[8,1728]{1,0:T(8,128)(2,1)S(1)} all-reduce(bf16[8,1728]{1,0:T(8,128)(2,1)S(1)} %multiply_convert_fusion.3), channel_id=1, replica_groups=mesh['gx'=16,'gy'=16] {'gy'}, use_global_device_ids=true, to_apply=%region_6.7 | all-reduce | flops 13824 | bytes 55296 | tf_op jit(solution)/shard_map/psum | solution.py:209
  416.1 4.2 collective-permute-start.27
  435.2 254.7 %all-reduce.13.cloned.1.call-done = (f32[64,864]{0,1:T(8,128)}, f32[64,5184]{1,0:T(8,128)}, f32[32,2592]{1,0:T(8,128)}) async-done(((f32[64,864]{0,1:T(8,128)}, f32[64,5184]{1,0:T(8,128)}, f32[32,2592]{1,0:T(8,128)}), (f32[64,864]{0,1:T(8,128)}, f32[64,5184]{1,0:T(8,128)}, f32[32,2592]{1,0:T(8,128)})) %all-reduce.13.cloned.1.call-update) | async-done | bytes 1880080 | tf_op jit(solution)/shard_map/psum | solution.py:213
  (1010 shorter events, 208.9 us)
Async XLA Ops:
  14.8 8.8 %collective-permute-start.2 = (bf16[32,4,8]{0,2,1:T(8,128)(2,1)S(1)}, bf16[32,4,8]{0,2,1:T(8,128)(2,1)S(1)}, u32[]{:S(2)}, u32[]{:S(2)}) collective-permute-start(bf16[32,4,8]{0,2,1:T(8,128)(2,1)S(1)} %get-tuple-element.241), channel_id=1, source_target_pairs={{0,1},{1,2},{2,3},{3,4},{4,5},{5,6},{6,7},{7,8},{8,9},{9,10},{10,1... | collective-permute-start | bytes 6152 | tf_op jit(solution)/shard_map/ppermute | solution.py:18
  17.9 5.5 collective-permute-start.3
  34.1 7.8 %collective-permute-start.4 = (bf16[64,1,4]{0,2,1:T(4,128)(2,1)S(1)}, bf16[64,1,4]{0,2,1:T(4,128)(2,1)S(1)}, u32[]{:S(2)}, u32[]{:S(2)}) collective-permute-start(bf16[64,1,4]{0,2,1:T(4,128)(2,1)S(1)} %get-tuple-element.309), channel_id=1, source_target_pairs={{0,1},{1,2},{2,3},{3,4},{4,5},{5,6},{6,7},{7,8},{8,9},{9,10},{10,1... | collective-permute-start | bytes 1544 | tf_op jit(solution)/shard_map/ppermute | solution.py:18
  40.0 5.5 collective-permute-start.5
  86.0 16.4 %all-to-all-start = ((bf16[8,16,16]{2,0,1:T(8,128)(2,1)}), bf16[8,16,16]{2,0,1:T(8,128)(2,1)S(1)}, u32[]{:S(2)}, u32[]{:S(2)}) async-start(bf16[8,16,16]{2,0,1:T(8,128)(2,1)} %copy.83), calls=%async_computation | async-start | bytes 65536 | tf_op jit(solution)/shard_map/all_to_all | solution.py:156
  108.0 6.1 collective-permute-start.8
  112.2 5.6 collective-permute-start.9
  134.4 6.2 collective-permute-start.12
  138.4 5.7 collective-permute-start.13
  157.6 5.1 collective-permute-start.14
  165.3 7.4 %collective-permute-start.16 = (bf16[32,6,16]{2,1,0:T(8,128)(2,1)S(1)}, bf16[32,6,16]{2,1,0:T(8,128)(2,1)S(1)}, u32[]{:S(2)}, u32[]{:S(2)}) collective-permute-start(bf16[32,6,16]{2,1,0:T(8,128)(2,1)S(1)} %get-tuple-element.138), channel_id=1, source_target_pairs={{0,1},{1,2},{2,3},{3,4},{4,5},{5,6},{6,7},{7,8},{8,9},{9,10},{10,1... | collective-permute-start | bytes 18440 | tf_op jit(solution)/shard_map/ppermute | solution.py:18
  169.3 6.2 collective-permute-start.17
  209.4 5.4 collective-permute-start.18
  217.7 7.8 %collective-permute-start.20 = (bf16[64,4,8]{2,1,0:T(4,128)(2,1)}, bf16[64,4,8]{2,1,0:T(4,128)(2,1)}, u32[]{:S(2)}, u32[]{:S(2)}) collective-permute-start(bf16[64,4,8]{2,1,0:T(4,128)(2,1)} %get-tuple-element.235), channel_id=1, source_target_pairs={{0,1},{1,2},{2,3},{3,4},{4,5},{5,6},{6,7},{7,8},{8,9},{9,10},{10,1... | collective-permute-start | bytes 12296 | tf_op jit(solution)/shard_map/ppermute | solution.py:18
  221.7 6.5 collective-permute-start.21
  270.0 38.6 %all-to-all-start.1 = ((f32[16,1,128]{2,1,0:T(1,128)}), f32[16,1,128]{2,1,0:T(1,128)S(1)}, u32[]{:S(2)}, u32[]{:S(2)}) async-start(f32[16,1,128]{2,1,0:T(1,128)} %reshape.1246), calls=%async_computation.1 | async-start | bytes 16384 | tf_op jit(solution)/shard_map/all_to_all | solution.py:196
  298.8 107.2 %reduce-scatter.2.cloned.1.call-start = ((), (), s32[]{:S(2)}) async-start(), calls=%async_computation.3 | async-start | bytes 69632 | tf_op jit(solution)/shard_map/reduce_scatter | solution.py:206
  314.0 6.5 collective-permute-start.22
  318.3 5.8 collective-permute-start.23
  335.0 354.9 %all-reduce.13.cloned.1.call-start = ((), (), s32[]{:S(2)}) async-start(), calls=%async_computation.4 | async-start | bytes 4259840 | tf_op jit(solution)/shard_map/psum | solution.py:213
  407.8 6.2 collective-permute-start.24
  409.1 4.9 collective-permute-start.25
  414.2 7.0 collective-permute-start.26
  416.1 6.2 collective-permute-start.27
  (184 other events, 3673.8 us)
Sparse Core Ops, SparseCore 0:
  335.1 68.1 reduce-scatter.1
  421.3 268.5 all-reduce.12
where the time goes:
time: 705 us; the launch traced here: 702 us
  waiting for transfers between devices  307 us (44%)
  starting transfers between devices  108 us (15%)
  blocking collectives  104 us (15%)
  matrix products  87.8 us (12%)
  local copies, waits for them, and re-layouts  58.3 us (8%)
  other arithmetic  19.2 us (3%)
  between operations  17.9 us (3%)
    psum x1, waiting for transfers between devices, per_device(): grad_encoder = lax.psum(local_encoder, ('gx', 'gy'))  255 us
    psum x1, blocking collectives, per_device(): lax.psum((part_bottom * scale_low).astype(jnp.bfloat16), 'gy')  70.2 us
    ppermute x14, starting transfers between devices, extended_2(): lax.ppermute(tail, axis, [(i, (i + 1) % count) for i in range(ends)])  46.2 us
    ppermute x14, waiting for transfers between devices, extended_2(): lax.ppermute(head, axis, [((i + 1) % count, i) for i in range(ends)])  34.1 us
    all_gather x1, blocking collectives, per_device(): whole_rows = lax.all_gather(col_ext, 'gx', axis=1, tiled=True)  33.5 us
    dot_general x108, matrix products, weight_grad(): lax.dot_general(error_flat, tap_piece(shifted_set, a, b, c, row_count, co...  33.3 us
    dot_general x108, matrix products, conv_backward(): lax.dot_general(weight[:, tap_number * in_chan:(tap_number + 1) * in_chan...  32.1 us
    reshape x108, local copies, waits for them, and re-layouts, tap_piece(): return tap_slice.reshape(source.shape[0], row_count * col_count * z_depth)  30.8 us
  transfers between devices with their start and end apart: 32, of which 16 were waited for; matrix products, arithmetic and copies ran while one was open for 4% of the time, Pallas kernels for 0%

commit v1 on v0

--- a/solution.py
+++ b/solution.py
@@ -206,7 +206,9 @@
     dpool_mid = lax.psum_scatter(
         partial_sum.astype(jnp.bfloat16), "gx", scatter_dimension=1, tiled=True
     ).astype(jnp.float32)
-    grad_bottom = lax.psum((part_bottom * scale_low).astype(jnp.bfloat16), "gy").astype(jnp.float32)
+    grad_bottom = jnp.sum(
+        lax.all_gather((part_bottom * scale_low).astype(jnp.bfloat16), "gy"), axis=0
+    ).astype(jnp.float32)
     dact_one = dcat_mid[low_chan:] + upsample(dpool_mid, depth_low) / 8.0
     err_one = (dact_one.reshape(mid_chan, -1) * silu_slope(pre_one)).astype(jnp.bfloat16)
     local_encoder = weight_grad(ext_pool, err_one, rows_mid, cols_mid, depth_mid) * scale_mid

time: 705 us -> 703 us (level)
  blocking collectives: 104 us -> 68.8 us
  waiting for transfers between devices: 307 us -> 341 us
    psum x1 -> x0, blocking collectives: 70.2 us -> none  [per_device(): lax.psum((part_bottom * scale_low).astype(jnp.bfloat16), 'gy')]
    all_gather x0 -> x1, blocking collectives: none -> 35.2 us  [per_device(): lax.all_gather((part_bottom * scale_low).astype(jnp.bfloat16), 'gy')]
    reduce_scatter x1, waiting for transfers between devices: 0.01 us -> 32.3 us  [per_device(): lax.psum_scatter(partial_sum.astype(jnp.bfloat16), 'gx', scatter_dimensio...]
  transfers between devices with their start and end apart: 32 -> 32, of which waited for: 16 -> 17; matrix products, arithmetic and copies ran while one was open for 4% -> 4% of each run, Pallas kernels for 0% -> 0%
where the time goes in v1:
time: 703 us; the launch traced here: 701 us
  waiting for transfers between devices  341 us (49%)
  starting transfers between devices  108 us (15%)
  matrix products  87.8 us (12%)
  blocking collectives  68.8 us (10%)
  local copies, waits for them, and re-layouts  58.3 us (8%)
  other arithmetic  19.3 us (3%)
  between operations  17.8 us (3%)
    psum x1, waiting for transfers between devices, per_device(): grad_encoder = lax.psum(local_encoder, ('gx', 'gy'))  255 us
    ppermute x14, starting transfers between devices, extended_2(): lax.ppermute(tail, axis, [(i, (i + 1) % count) for i in range(ends)])  47.3 us
    ppermute x14, waiting for transfers between devices, extended_2(): lax.ppermute(head, axis, [((i + 1) % count, i) for i in range(ends)])  35.3 us
    all_gather x1, blocking collectives, per_device(): lax.all_gather((part_bottom * scale_low).astype(jnp.bfloat16), 'gy')  35.2 us
    all_gather x1, blocking collectives, per_device(): whole_rows = lax.all_gather(col_ext, 'gx', axis=1, tiled=True)  33.5 us
    dot_general x108, matrix products, weight_grad(): lax.dot_general(error_flat, tap_piece(shifted_set, a, b, c, row_count, co...  33.3 us
    reduce_scatter x1, waiting for transfers between devices, per_device(): lax.psum_scatter(partial_sum.astype(jnp.bfloat16), 'gx', scatter_dimensio...  32.3 us
    dot_general x108, matrix products, conv_backward(): lax.dot_general(weight[:, tap_number * in_chan:(tap_number + 1) * in_chan...  32.1 us
  transfers between devices with their start and end apart: 32, of which 17 were waited for; matrix products, arithmetic and copies ran while one was open for 4% of the time, Pallas kernels for 0%

profile of v1, /device:TPU:4, one launch (start us, length us, event | category | flops | bytes accessed | tf_op | source)
XLA Modules:
  0.0 700.5 jit_solution(5753229995095539862)
XLA Ops:
  14.8 3.1 collective-permute-start.2
  34.1 5.8 collective-permute-start.4
  41.9 3.5 collective-permute-done.5
  45.5 33.5 %all_gather.7 = bf16[64,16,24]{0,2,1:T(8,128)(2,1)S(1)} all-gather(bf16[64,1,24]{0,2,1:T(8,128)(2,1)S(1)} %pad_maximum_fusion.21), channel_id=1, replica_groups=mesh['gx'=16,'gy'=16] {'gx'}, dimensions={1}, use_global_device_ids=true | all-gather | bytes 52224 | tf_op jit(solution)/shard_map/all_gather | solution.py:149
  86.0 6.4 all-to-all-start
  92.6 9.9 %all-to-all-done = bf16[8,16,16]{2,0,1:T(8,128)(2,1)S(1)} async-done(((bf16[8,16,16]{2,0,1:T(8,128)(2,1)}), bf16[8,16,16]{2,0,1:T(8,128)(2,1)S(1)}, u32[]{:S(2)}, u32[]{:S(2)}) %all-to-all-start) | async-done | bytes 4128 | tf_op jit(solution)/shard_map/all_to_all | solution.py:156
  108.0 4.2 collective-permute-start.8
  114.2 3.7 collective-permute-done.9
  127.1 3.1 collective-permute-start.10
  134.4 4.1 collective-permute-start.12
  140.6 3.6 collective-permute-done.13
  157.7 3.4 collective-permute-start.14
  165.3 4.1 collective-permute-start.16
  209.4 3.1 collective-permute-start.18
  217.7 4.0 collective-permute-start.20
  270.0 28.7 %all-to-all-start.1 = ((f32[16,1,128]{2,1,0:T(1,128)}), f32[16,1,128]{2,1,0:T(1,128)S(1)}, u32[]{:S(2)}, u32[]{:S(2)}) async-start(f32[16,1,128]{2,1,0:T(1,128)} %reshape.1603), calls=%async_computation.1 | async-start | bytes 16384 | tf_op jit(solution)/shard_map/all_to_all | solution.py:196
  300.3 8.3 %all-to-all-done.1 = f32[16,1,128]{2,1,0:T(1,128)S(1)} async-done(((f32[16,1,128]{2,1,0:T(1,128)}), f32[16,1,128]{2,1,0:T(1,128)S(1)}, u32[]{:S(2)}, u32[]{:S(2)}) %all-to-all-start.1) | async-done | bytes 8224 | tf_op jit(solution)/shard_map/all_to_all | solution.py:196
  314.2 4.3 collective-permute-start.22
  320.5 3.8 collective-permute-done.23
  335.2 35.2 %all_gather.8 = bf16[16,8,1728]{2,1,0:T(8,128)(2,1)S(1)} all-gather(bf16[1,8,1728]{2,1,0:T(8,128)(2,1)S(1)} %multiply_convert_fusion.3), channel_id=1, replica_groups=mesh['gx'=16,'gy'=16] {'gy'}, dimensions={0}, use_global_device_ids=true | all-gather | bytes 470016 | tf_op jit(solution)/shard_map/all_gather | solution.py:210
  371.1 32.3 %reduce-scatter.2.cloned.1.call-done = bf16[64,1,16]{0,2,1:T(8,128)(2,1)} async-done(((bf16[64,16,16]{0,2,1:T(8,128)(2,1)}), bf16[64,1,16]{0,2,1:T(8,128)(2,1)}) %reduce-scatter.2.cloned.1.call-update) | async-done | bytes 2064 | tf_op jit(solution)/shard_map/reduce_scatter | solution.py:206
  411.7 3.1 collective-permute-start.26
  414.8 3.0 collective-permute-start.27
  433.8 254.7 %all-reduce.13.cloned.1.call-done = (f32[64,864]{0,1:T(8,128)}, f32[64,5184]{1,0:T(8,128)}, f32[32,2592]{1,0:T(8,128)}) async-done(((f32[64,864]{0,1:T(8,128)}, f32[64,5184]{1,0:T(8,128)}, f32[32,2592]{1,0:T(8,128)}), (f32[64,864]{0,1:T(8,128)}, f32[64,5184]{1,0:T(8,128)}, f32[32,2592]{1,0:T(8,128)})) %all-reduce.13.cloned.1.call-update) | async-done | bytes 1880080 | tf_op jit(solution)/shard_map/psum | solution.py:215
  (1011 shorter events, 213.7 us)
Async XLA Ops:
  14.8 8.8 %collective-permute-start.2 = (bf16[32,4,8]{0,2,1:T(8,128)(2,1)S(1)}, bf16[32,4,8]{0,2,1:T(8,128)(2,1)S(1)}, u32[]{:S(2)}, u32[]{:S(2)}) collective-permute-start(bf16[32,4,8]{0,2,1:T(8,128)(2,1)S(1)} %get-tuple-element.241), channel_id=1, source_target_pairs={{0,1},{1,2},{2,3},{3,4},{4,5},{5,6},{6,7},{7,8},{8,9},{9,10},{10,1... | collective-permute-start | bytes 6152 | tf_op jit(solution)/shard_map/ppermute | solution.py:18
  17.9 5.5 collective-permute-start.3
  34.1 7.8 %collective-permute-start.4 = (bf16[64,1,4]{0,2,1:T(4,128)(2,1)S(1)}, bf16[64,1,4]{0,2,1:T(4,128)(2,1)S(1)}, u32[]{:S(2)}, u32[]{:S(2)}) collective-permute-start(bf16[64,1,4]{0,2,1:T(4,128)(2,1)S(1)} %get-tuple-element.309), channel_id=1, source_target_pairs={{0,1},{1,2},{2,3},{3,4},{4,5},{5,6},{6,7},{7,8},{8,9},{9,10},{10,1... | collective-permute-start | bytes 1544 | tf_op jit(solution)/shard_map/ppermute | solution.py:18
  40.0 5.5 collective-permute-start.5
  86.0 16.4 %all-to-all-start = ((bf16[8,16,16]{2,0,1:T(8,128)(2,1)}), bf16[8,16,16]{2,0,1:T(8,128)(2,1)S(1)}, u32[]{:S(2)}, u32[]{:S(2)}) async-start(bf16[8,16,16]{2,0,1:T(8,128)(2,1)} %copy.83), calls=%async_computation | async-start | bytes 65536 | tf_op jit(solution)/shard_map/all_to_all | solution.py:156
  108.0 6.1 collective-permute-start.8
  112.2 5.6 collective-permute-start.9
  134.4 6.2 collective-permute-start.12
  138.4 5.7 collective-permute-start.13
  157.7 5.1 collective-permute-start.14
  165.3 7.4 %collective-permute-start.16 = (bf16[32,6,16]{2,1,0:T(8,128)(2,1)S(1)}, bf16[32,6,16]{2,1,0:T(8,128)(2,1)S(1)}, u32[]{:S(2)}, u32[]{:S(2)}) collective-permute-start(bf16[32,6,16]{2,1,0:T(8,128)(2,1)S(1)} %get-tuple-element.138), channel_id=1, source_target_pairs={{0,1},{1,2},{2,3},{3,4},{4,5},{5,6},{6,7},{7,8},{8,9},{9,10},{10,1... | collective-permute-start | bytes 18440 | tf_op jit(solution)/shard_map/ppermute | solution.py:18
  169.3 6.2 collective-permute-start.17
  209.4 5.4 collective-permute-start.18
  217.7 7.8 %collective-permute-start.20 = (bf16[64,4,8]{2,1,0:T(4,128)(2,1)}, bf16[64,4,8]{2,1,0:T(4,128)(2,1)}, u32[]{:S(2)}, u32[]{:S(2)}) collective-permute-start(bf16[64,4,8]{2,1,0:T(4,128)(2,1)} %get-tuple-element.235), channel_id=1, source_target_pairs={{0,1},{1,2},{2,3},{3,4},{4,5},{5,6},{6,7},{7,8},{8,9},{9,10},{10,1... | collective-permute-start | bytes 12296 | tf_op jit(solution)/shard_map/ppermute | solution.py:18
  221.7 6.5 collective-permute-start.21
  270.0 38.6 %all-to-all-start.1 = ((f32[16,1,128]{2,1,0:T(1,128)}), f32[16,1,128]{2,1,0:T(1,128)S(1)}, u32[]{:S(2)}, u32[]{:S(2)}) async-start(f32[16,1,128]{2,1,0:T(1,128)} %reshape.1603), calls=%async_computation.1 | async-start | bytes 16384 | tf_op jit(solution)/shard_map/all_to_all | solution.py:196
  298.8 104.7 %reduce-scatter.2.cloned.1.call-start = ((), (), s32[]{:S(2)}) async-start(), calls=%async_computation.3 | async-start | bytes 69632 | tf_op jit(solution)/shard_map/reduce_scatter | solution.py:206
  314.2 6.4 collective-permute-start.22
  318.5 5.8 collective-permute-start.23
  335.1 353.4 %all-reduce.13.cloned.1.call-start = ((), (), s32[]{:S(2)}) async-start(), calls=%async_computation.4 | async-start | bytes 4259840 | tf_op jit(solution)/shard_map/psum | solution.py:215
  405.3 6.2 collective-permute-start.24
  406.6 4.9 collective-permute-start.25
  411.7 7.0 collective-permute-start.26
  414.8 6.2 collective-permute-start.27
  (184 other events, 3553.3 us)
Sparse Core Ops, SparseCore 0:
  335.3 68.1 reduce-scatter.1
  418.8 269.6 all-reduce.12
